TPU v7x, 128 devices: a whole 4x4x4 slice. The times are simulated.
128 devices in a mesh: rows: 8 (over z, core), cols: 16 (over y, x).
Axes of the slice: x: 4, y: 4, z: 4, core: 2. Of those that a mesh axis runs over, the one named last changes fastest.
Arguments:
- pivot_rhs: float32 [4, 4096, 1024], P(None, 'cols'), may hold values from -6 to 6
- bound_sol: bfloat16 [16384, 1024], P('rows'), may hold values from -6 to 6
- border_tiles: bfloat16 [16384, 4, 4096], P('rows', None, 'cols'), may hold values from -0.046875 to 0.046875
- lower_tiles: bfloat16 [6, 4096, 4096], P(None, 'rows', 'cols'), may hold values from -0.09375 to 0.09375
- inverse_diag: bfloat16 [4, 4096, 4096], P(None, 'cols', 'rows'), may hold values from -0.09375 to 0.09375
- owner_map: int32 [128, 128, 1], P(('rows', 'cols')), may hold values from 0 to 127; in each aligned block of 128 rows (0 to 127, 128 to 255, ..., all dimensions but the last counted through in order) at most 2 rows name the same one
Outputs:
- child_rows: float32 [32768, 1024], P(('rows', 'cols'))
Inputs may be any that keep to these rules, and one draw needn't show every extreme that they name: `owner_map`: among the rows of one device (one index of the first dimension), no owner is named more than 2 times, a bound that some block reaches; every owner is named somewhere.
All inputs are finite; a program needn't handle non-finite values.
Results may differ from a plain program's by a relative error of at most 0.008.
Values may be sent and summed in bfloat16 or wider, within the bound.
No kernel may reach another device: no remote copies, remote signals or barrier semaphores. Data moves between devices by JAX's collectives and lax.ppermute only.
A program may use at most 64 MiB of HBM per device.

v0:
```python
import jax
import jax.numpy as jnp
from jax import lax
from jax.sharding import PartitionSpec as P


def pair_slot(later, earlier):
    return later * (later - 1) // 2 + earlier


def pack_rows(rows_here, owners, devices, most):
    onehot = (owners[:, None] == jnp.arange(devices, dtype=jnp.int32)[None, :]).astype(jnp.int32)
    ranks = jnp.cumsum(onehot, axis=0) - onehot
    slots = jnp.sum(ranks * onehot, axis=1)
    target = owners * most + slots
    select = (jnp.arange(devices * most, dtype=jnp.int32)[:, None] == target[None, :]).astype(
        jnp.float32
    )
    return jnp.dot(
        select, rows_here, precision=lax.Precision.HIGHEST, preferred_element_type=jnp.float32
    )


def tile_term(tile, vectors):
    return lax.dot_general(
        tile, vectors, (((0,), (0,)), ((), ())), preferred_element_type=jnp.float32
    )


def local(pivot_rhs, bound_sol, border_tiles, lower_tiles, inverse_diag, owner_map):
    devices = lax.axis_size("rows") * lax.axis_size("cols")
    blocks = pivot_rhs.shape[0]
    width_here = pivot_rhs.shape[1]
    sources = pivot_rhs.shape[2]
    rows_dev = owner_map.shape[1]
    most = max(2, 2 * rows_dev // devices)
    border_part = lax.dot_general(
        border_tiles, bound_sol, (((0,), (0,)), ((), ())), preferred_element_type=jnp.float32
    )
    pending = []
    border_full = lax.psum(border_part, "rows")
    for k in range(blocks):
        pending.append(jnp.zeros((width_here, sources), jnp.float32))
    rounded = [None] * blocks
    own_rows = [None] * blocks
    for k in reversed(range(blocks)):
        local_sum = pending[k]
        for j in range(k + 1, blocks):
            local_sum = local_sum + tile_term(lower_tiles[pair_slot(j, k)], rounded[j])
        summed = lax.psum(local_sum, "rows")
        summed = summed + border_full[k]
        residual = (pivot_rhs[k] - summed).astype(jnp.bfloat16)
        inverse_here = inverse_diag[k]
        solved_here = lax.psum_scatter(
            tile_term(inverse_here, residual), "cols", scatter_dimension=0, tiled=True
        )
        own_rows[k] = solved_here
        if k > 0:
            rounded[k] = lax.all_gather(
                solved_here.astype(jnp.bfloat16), "cols", axis=0, tiled=True
            )
    rows_here = jnp.concatenate(own_rows, axis=0)
    owners = owner_map[0, :, 0]
    buffer = pack_rows(rows_here, owners, devices, most).reshape(devices, most, sources)
    received = lax.all_to_all(buffer, ("rows", "cols"), split_axis=0, concat_axis=0, tiled=True)
    return received.reshape(devices * most, sources)


def solution(mesh):
    placed = (
        P(None, "cols", None),
        P("rows", None),
        P("rows", None, "cols"),
        P(None, "rows", "cols"),
        P(None, "cols", "rows"),
        P(("rows", "cols"), None, None),
    )
    return jax.shard_map(
        local, mesh=mesh, in_specs=placed, out_specs=P(("rows", "cols"), None), check_vma=False
    )
```

profile of v0, /device:TPU:1, one launch (start us, length us, event | category | flops | bytes accessed | tf_op | source)
XLA Modules:
  0.0 773.4 jit_solution(16388644528442897463)
XLA Ops:
  6.5 10.0 %fusion = f32[4,256,1024]{2,1,0:T(8,128)} fusion(bf16[2048,1024]{1,0:T(8,128)(2,1)} %param.7, bf16[2048,4,256]{2,1,0:T(4,128)(2,1)} %param.8), kind=kOutput, calls=%fused_computation | convolution fusion | flops 4294967296 | bytes 12582912 | tf_op jit(solution)/shard_map/dot_general | solution.py:37
  16.6 74.5 %all-reduce.5.cloned.1.call-done = f32[4,256,1024]{2,1,0:T(8,128)} async-done(((f32[4,256,1024]{2,1,0:T(8,128)}), f32[4,256,1024]{2,1,0:T(8,128)}) %all-reduce.5.cloned.1.call-update) | async-done | bytes 4194320 | tf_op jit(solution)/shard_map/psum | solution.py:41
  91.2 2.1 convolution_bitcast_fusion.3
  93.2 1.8 copy.28
  95.1 74.3 %reduce-scatter.13.cloned.1.call-done = f32[32,1024]{1,0:T(8,128)} async-done(((f32[512,1024]{1,0:T(8,128)}), f32[32,1024]{1,0:T(8,128)}) %reduce-scatter.13.cloned.1.call-update) | async-done | bytes 131088 | tf_op jit(solution)/shard_map/reduce_scatter | solution.py:54
  169.5 1.5 convert_element_type.31
  171.1 42.9 %all-gather.4.cloned.1.call-done = bf16[512,1024]{1,0:T(8,128)(2,1)} async-done(((bf16[32,1024]{1,0:T(8,128)(2,1)}), bf16[512,1024]{1,0:T(8,128)(2,1)}) %all-gather.4.cloned.1.call-update) | async-done | bytes 1048592 | tf_op jit(solution)/shard_map/all_gather | solution.py:59
  214.0 2.7 convolution_bitcast_fusion.4
  216.8 61.5 %all-reduce.7.cloned.1.call-done = f32[256,1024]{1,0:T(8,128)} async-done(((f32[256,1024]{1,0:T(8,128)}), f32[256,1024]{1,0:T(8,128)}) %all-reduce.7.cloned.1.call-update) | async-done | bytes 1048592 | tf_op jit(solution)/shard_map/psum | solution.py:50
  278.3 2.5 convolution_bitcast_fusion.2
  280.8 1.8 copy.30
  282.7 73.8 %reduce-scatter.15.cloned.1.call-done = f32[32,1024]{1,0:T(8,128)} async-done(((f32[512,1024]{1,0:T(8,128)}), f32[32,1024]{1,0:T(8,128)}) %reduce-scatter.15.cloned.1.call-update) | async-done | bytes 131088 | tf_op jit(solution)/shard_map/reduce_scatter | solution.py:54
  356.5 1.5 convert_element_type.33
  358.1 42.5 %all-gather.6.cloned.1.call-done = bf16[512,1024]{1,0:T(8,128)(2,1)} async-done(((bf16[32,1024]{1,0:T(8,128)(2,1)}), bf16[512,1024]{1,0:T(8,128)(2,1)}) %all-gather.6.cloned.1.call-update) | async-done | bytes 1048592 | tf_op jit(solution)/shard_map/all_gather | solution.py:59
  400.6 1.7 fusion.35
  402.4 2.4 fusion.4
  404.9 61.5 %all-reduce.9.cloned.1.call-done = f32[256,1024]{1,0:T(8,128)} async-done(((f32[256,1024]{1,0:T(8,128)}), f32[256,1024]{1,0:T(8,128)}) %all-reduce.9.cloned.1.call-update) | async-done | bytes 1048592 | tf_op jit(solution)/shard_map/psum | solution.py:50
  466.4 2.5 convolution_bitcast_fusion.1
  468.8 1.8 copy.32
  470.8 73.8 %reduce-scatter.17.cloned.1.call-done = f32[32,1024]{1,0:T(8,128)} async-done(((f32[512,1024]{1,0:T(8,128)}), f32[32,1024]{1,0:T(8,128)}) %reduce-scatter.17.cloned.1.call-update) | async-done | bytes 131088 | tf_op jit(solution)/shard_map/reduce_scatter | solution.py:54
  544.6 1.5 convert_element_type.35
  546.2 42.9 %all-gather.8.cloned.1.call-done = bf16[512,1024]{1,0:T(8,128)(2,1)} async-done(((bf16[32,1024]{1,0:T(8,128)(2,1)}), bf16[512,1024]{1,0:T(8,128)(2,1)}) %all-gather.8.cloned.1.call-update) | async-done | bytes 1048592 | tf_op jit(solution)/shard_map/all_gather | solution.py:59
  589.1 1.7 fusion.31
  590.8 1.4 convolution_add_fusion.1
  592.3 2.4 fusion.3
  595.0 61.3 %all-reduce.11.cloned.1.call-done = f32[256,1024]{1,0:T(8,128)} async-done(((f32[256,1024]{1,0:T(8,128)}), f32[256,1024]{1,0:T(8,128)}) %all-reduce.11.cloned.1.call-update) | async-done | bytes 1048592 | tf_op jit(solution)/shard_map/psum | solution.py:50
  656.3 2.5 convolution_bitcast_fusion
  658.8 1.9 copy.34
  661.8 72.8 %reduce-scatter.19.cloned.1.call-done = f32[32,1024]{1,0:T(8,128)} async-done(((f32[512,1024]{1,0:T(8,128)}), f32[32,1024]{1,0:T(8,128)}) %reduce-scatter.19.cloned.1.call-update) | async-done | bytes 131088
  734.6 1.1 copy.35
  737.3 27.9 %all_to_all.5 = f32[128,2,1024]{2,1,0:T(2,128)S(1)} all-to-all(f32[128,2,1024]{2,1,0:T(2,128)S(1)} %reshape.16), channel_id=1, replica_groups=mesh['rows'=8,'cols'=16] {'rows','cols'}, dimensions={0} | all-to-all | bytes 2097152 | tf_op jit(solution)/shard_map/all_to_all | solution.py:65
  765.2 1.7 reshape.17
  (43 shorter events, 3.4 us)
Async XLA Ops:
  6.5 84.6 %all-reduce.5.cloned.1.call-start = ((), (), s32[]{:S(2)}) async-start(), calls=%async_computation.5 | async-start | bytes 8388608 | tf_op jit(solution)/shard_map/psum | solution.py:41
  16.6 152.9 %reduce-scatter.13.cloned.1.call-start = ((), (), s32[]{:S(2)}) async-start(), calls=%async_computation.12 | async-start | bytes 2228224 | tf_op jit(solution)/shard_map/reduce_scatter | solution.py:54
  95.1 118.9 %all-gather.4.cloned.1.call-start = ((), (), s32[]{:S(2)}) async-start(), calls=%async_computation.6 | async-start | bytes 1114112 | tf_op jit(solution)/shard_map/all_gather | solution.py:59
  171.0 107.3 %all-reduce.7.cloned.1.call-start = ((), (), s32[]{:S(2)}) async-start(), calls=%async_computation.7 | async-start | bytes 2097152 | tf_op jit(solution)/shard_map/psum | solution.py:50
  216.7 139.7 %reduce-scatter.15.cloned.1.call-start = ((), (), s32[]{:S(2)}) async-start(), calls=%async_computation.13 | async-start | bytes 2228224 | tf_op jit(solution)/shard_map/reduce_scatter | solution.py:54
  280.8 121.6 %copy-start = (bf16[512,1024]{1,0:T(8,128)(2,1)S(1)}, bf16[512,1024]{1,0:T(8,128)(2,1)}, u32[]{:S(2)}) copy-start(bf16[512,1024]{1,0:T(8,128)(2,1)} %all-gather.4.cloned.1.call-done) | copy-start | bytes 3145732
  282.6 118.0 %all-gather.6.cloned.1.call-start = ((), (), s32[]{:S(2)}) async-start(), calls=%async_computation.8 | async-start | bytes 1114112 | tf_op jit(solution)/shard_map/all_gather | solution.py:59
  358.0 108.3 %all-reduce.9.cloned.1.call-start = ((), (), s32[]{:S(2)}) async-start(), calls=%async_computation.9 | async-start | bytes 2097152 | tf_op jit(solution)/shard_map/psum | solution.py:50
  404.8 139.7 %reduce-scatter.17.cloned.1.call-start = ((), (), s32[]{:S(2)}) async-start(), calls=%async_computation.14 | async-start | bytes 2228224 | tf_op jit(solution)/shard_map/reduce_scatter | solution.py:54
  470.7 120.1 %copy-start.1 = (bf16[512,1024]{1,0:T(8,128)(2,1)S(1)}, bf16[512,1024]{1,0:T(8,128)(2,1)}, u32[]{:S(2)}) copy-start(bf16[512,1024]{1,0:T(8,128)(2,1)} %all-gather.6.cloned.1.call-done) | copy-start | bytes 3145732
  470.7 118.4 %all-gather.8.cloned.1.call-start = ((), (), s32[]{:S(2)}) async-start(), calls=%async_computation.10 | async-start | bytes 1114112 | tf_op jit(solution)/shard_map/all_gather | solution.py:59
  546.1 110.1 %all-reduce.11.cloned.1.call-start = ((), (), s32[]{:S(2)}) async-start(), calls=%async_computation.11 | async-start | bytes 2097152 | tf_op jit(solution)/shard_map/psum | solution.py:50
  594.7 139.9 %reduce-scatter.19.cloned.1.call-start = ((), (), s32[]{:S(2)}) async-start(), calls=%async_computation.15 | async-start | bytes 2228224
  658.8 1.9 copy-start.5
  658.8 2.4 copy-start.2
  658.8 2.6 copy-start.3
  658.8 2.8 copy-start.4
Sparse Core Ops, SparseCore 0:
  16.7 74.4 all-reduce.4
  95.2 74.1 reduce-scatter.12
  171.8 42.1 all-gather.3
  216.9 61.3 all-reduce.6
  282.8 73.6 reduce-scatter.14
  358.5 42.1 all-gather.5
  404.9 61.3 all-reduce.8
  470.8 73.6 reduce-scatter.16
  546.9 42.0 all-gather.7
  594.8 61.3 all-reduce.10
  660.8 73.7 reduce-scatter.18
where the time goes:
time: 774 us; the launch traced here: 773 us
  waiting for transfers between devices  682 us (88%)
  matrix products  33 us (4%)
  blocking collectives  27.9 us (4%)
  between operations  13.4 us (2%)
  local copies, waits for them, and re-layouts  11.4 us (1%)
    reduce_scatter x3, waiting for transfers between devices, local(): lax.psum_scatter(tile_term(inverse_here, residual), 'cols', scatter_dimen...  222 us
    psum x3, waiting for transfers between devices, local(): summed = lax.psum(local_sum, 'rows')  184 us
    all_gather x3, waiting for transfers between devices, local(): lax.all_gather(solved_here.astype(jnp.bfloat16), 'cols', axis=0, tiled=True)  128 us
    psum x1, waiting for transfers between devices, local(): border_full = lax.psum(border_part, 'rows')  74.5 us
    unnamed x12, waiting for transfers between devices  73 us
    all_to_all x1, blocking collectives, local(): lax.all_to_all(buffer, ('rows', 'cols'), split_axis=0, concat_axis=0, til...  27.9 us
    dot_general x10, matrix products, tile_term(): lax.dot_general(tile, vectors, (((0,), (0,)), ((), ())), preferred_elemen...  22 us
  transfers between devices with their start and end apart: 11, of which 11 were waited for; matrix products, arithmetic and copies ran while one was open for 0% of the time, Pallas kernels for 0%

commit v1 on v0

--- a/solution.py
+++ b/solution.py
@@ -2,6 +2,13 @@
 import jax.numpy as jnp
 from jax import lax
 from jax.sharding import PartitionSpec as P
+
+supply_all_the_rings = lambda local_block, shard_axis: jnp.concatenate(
+    jax.lax.all_to_all(
+        jnp.stack([local_block for _ in range(jax.lax.axis_size(shard_axis))], 0), shard_axis, 0, 0
+    ),
+    axis=0,
+)
 
 
 def pair_slot(later, earlier):
@@ -56,9 +63,7 @@
         )
         own_rows[k] = solved_here
         if k > 0:
-            rounded[k] = lax.all_gather(
-                solved_here.astype(jnp.bfloat16), "cols", axis=0, tiled=True
-            )
+            rounded[k] = supply_all_the_rings(solved_here.astype(jnp.bfloat16), shard_axis="cols")
     rows_here = jnp.concatenate(own_rows, axis=0)
     owners = owner_map[0, :, 0]
     buffer = pack_rows(rows_here, owners, devices, most).reshape(devices, most, sources)

time: 774 us -> 701 us (0.906)
  waiting for transfers between devices: 682 us -> 554 us
  blocking collectives: 27.9 us -> 83 us
    all_gather x3 -> x0, waiting for transfers between devices: 128 us -> none  [local(): lax.all_gather(solved_here.astype(jnp.bfloat16), 'cols', axis=0, tiled=True)]
    all_to_all x0 -> x3, blocking collectives: none -> 55.2 us  [jax.lax.all_to_all(jnp.stack([local_block for _ in range(jax.lax.axis_siz...]
    unnamed x12 -> x9, waiting for transfers between devices: 73 us -> 72.9 us
  transfers between devices with their start and end apart: 11 -> 8, of which waited for: 11 -> 8; matrix products, arithmetic and copies ran while one was open for 0% -> 0% of each run, Pallas kernels for 0% -> 0%
where the time goes in v1:
time: 701 us
  waiting for transfers between devices  554 us (79%)
  blocking collectives  83 us (12%)
  matrix products  33.3 us (5%)
  between operations  13.7 us (2%)
  local copies, waits for them, and re-layouts  12.9 us (2%)
    reduce_scatter x3, waiting for transfers between devices, local(): lax.psum_scatter(tile_term(inverse_here, residual), 'cols', scatter_dimen...  222 us
    psum x3, waiting for transfers between devices, local(): summed = lax.psum(local_sum, 'rows')  185 us
    psum x1, waiting for transfers between devices, local(): border_full = lax.psum(border_part, 'rows')  74.5 us
    unnamed x9, waiting for transfers between devices  72.9 us
    all_to_all x3, blocking collectives, jax.lax.all_to_all(jnp.stack([local_block for _ in range(jax.lax.axis_siz...  55.2 us
    all_to_all x1, blocking collectives, local(): lax.all_to_all(buffer, ('rows', 'cols'), split_axis=0, concat_axis=0, til...  27.9 us
    dot_general x10, matrix products, tile_term(): lax.dot_general(tile, vectors, (((0,), (0,)), ((), ())), preferred_elemen...  22.3 us
  transfers between devices with their start and end apart: 8, of which 8 were waited for; matrix products, arithmetic and copies ran while one was open for 0% of the time, Pallas kernels for 0%

profile of v1, /device:TPU:1, one launch (start us, length us, event | category | flops | bytes accessed | tf_op | source)
XLA Modules:
  0.0 700.8 jit_solution(11687962205961455212)
XLA Ops:
  6.5 10.0 %fusion = f32[4,256,1024]{2,1,0:T(8,128)} fusion(bf16[2048,1024]{1,0:T(8,128)(2,1)} %param.7, bf16[2048,4,256]{2,1,0:T(4,128)(2,1)} %param.8), kind=kOutput, calls=%fused_computation | convolution fusion | flops 4294967296 | bytes 12582912 | tf_op jit(solution)/shard_map/dot_general | solution.py:44
  16.6 74.5 %all-reduce.5.cloned.1.call-done = f32[4,256,1024]{2,1,0:T(8,128)} async-done(((f32[4,256,1024]{2,1,0:T(8,128)}), f32[4,256,1024]{2,1,0:T(8,128)}) %all-reduce.5.cloned.1.call-update) | async-done | bytes 4194320 | tf_op jit(solution)/shard_map/psum | solution.py:48
  91.1 2.1 convolution_bitcast_fusion.3
  93.2 1.9 copy.31
  95.2 74.4 %reduce-scatter.13.cloned.1.call-done = f32[32,1024]{1,0:T(8,128)} async-done(((f32[512,1024]{1,0:T(8,128)}), f32[32,1024]{1,0:T(8,128)}) %reduce-scatter.13.cloned.1.call-update) | async-done | bytes 131088 | tf_op jit(solution)/shard_map/reduce_scatter | solution.py:61
  169.5 0.9 convert_element_type.31
  170.6 18.4 %all_to_all.20 = bf16[16,32,1024]{2,1,0:T(8,128)(2,1)S(1)} all-to-all(bf16[16,32,1024]{2,1,0:T(8,128)(2,1)S(1)} %stack.6), channel_id=1, replica_groups=mesh['rows'=8,'cols'=16] {'cols'}, dimensions={0} | all-to-all | bytes 2097152 | tf_op jit(solution)/shard_map/all_to_all | solution.py:7
  188.9 2.4 convolution_bitcast_fusion.4
  191.4 61.7 %all-reduce.7.cloned.1.call-done = f32[256,1024]{1,0:T(8,128)} async-done(((f32[256,1024]{1,0:T(8,128)}), f32[256,1024]{1,0:T(8,128)}) %all-reduce.7.cloned.1.call-update) | async-done | bytes 1048592 | tf_op jit(solution)/shard_map/psum | solution.py:57
  253.1 2.5 convolution_bitcast_fusion.2
  255.6 1.9 copy.33
  257.5 73.8 %reduce-scatter.15.cloned.1.call-done = f32[32,1024]{1,0:T(8,128)} async-done(((f32[512,1024]{1,0:T(8,128)}), f32[32,1024]{1,0:T(8,128)}) %reduce-scatter.15.cloned.1.call-update) | async-done | bytes 131088 | tf_op jit(solution)/shard_map/reduce_scatter | solution.py:61
  331.3 0.9 convert_element_type.33
  332.3 18.5 %all_to_all.21 = bf16[16,32,1024]{2,1,0:T(8,128)(2,1)S(1)} all-to-all(bf16[16,32,1024]{2,1,0:T(8,128)(2,1)S(1)} %stack.7), channel_id=1, replica_groups=mesh['rows'=8,'cols'=16] {'cols'}, dimensions={0} | all-to-all | bytes 2097152 | tf_op jit(solution)/shard_map/all_to_all | solution.py:7
  350.8 1.4 fusion.35
  352.2 2.4 fusion.4
  354.7 61.7 %all-reduce.9.cloned.1.call-done = f32[256,1024]{1,0:T(8,128)} async-done(((f32[256,1024]{1,0:T(8,128)}), f32[256,1024]{1,0:T(8,128)}) %all-reduce.9.cloned.1.call-update) | async-done | bytes 1048592 | tf_op jit(solution)/shard_map/psum | solution.py:57
  416.4 3.8 convolution_bitcast_fusion.1
  420.2 2.9 copy.35
  423.2 73.8 %reduce-scatter.17.cloned.1.call-done = f32[32,1024]{1,0:T(8,128)} async-done(((f32[512,1024]{1,0:T(8,128)}), f32[32,1024]{1,0:T(8,128)}) %reduce-scatter.17.cloned.1.call-update) | async-done | bytes 131088 | tf_op jit(solution)/shard_map/reduce_scatter | solution.py:61
  498.0 18.3 %all_to_all.22 = bf16[16,32,1024]{2,1,0:T(8,128)(2,1)S(1)} all-to-all(bf16[16,32,1024]{2,1,0:T(8,128)(2,1)S(1)} %stack.8), channel_id=1, replica_groups=mesh['rows'=8,'cols'=16] {'cols'}, dimensions={0} | all-to-all | bytes 2097152 | tf_op jit(solution)/shard_map/all_to_all | solution.py:7
  516.4 1.4 fusion.31
  517.8 1.4 convolution_add_fusion.1
  519.3 2.4 fusion.3
  521.9 61.5 %all-reduce.11.cloned.1.call-done = f32[256,1024]{1,0:T(8,128)} async-done(((f32[256,1024]{1,0:T(8,128)}), f32[256,1024]{1,0:T(8,128)}) %all-reduce.11.cloned.1.call-update) | async-done | bytes 1048592 | tf_op jit(solution)/shard_map/psum | solution.py:57
  583.4 2.4 convolution_bitcast_fusion
  585.9 1.9 copy.37
  588.9 72.8 %reduce-scatter.19.cloned.1.call-done = f32[32,1024]{1,0:T(8,128)} async-done(((f32[512,1024]{1,0:T(8,128)}), f32[32,1024]{1,0:T(8,128)}) %reduce-scatter.19.cloned.1.call-update) | async-done | bytes 131088
  661.7 1.1 copy.38
  662.8 1.0 fusion.20
  664.4 27.9 %all_to_all.23 = f32[128,2,1024]{2,1,0:T(2,128)S(1)} all-to-all(f32[128,2,1024]{2,1,0:T(2,128)S(1)} %reshape.34), channel_id=1, replica_groups=mesh['rows'=8,'cols'=16] {'rows','cols'}, dimensions={0} | all-to-all | bytes 2097152 | tf_op jit(solution)/shard_map/all_to_all | solution.py:70
  692.3 1.7 reshape.35
  (38 shorter events, 3.5 us)
Async XLA Ops:
  6.5 84.6 %all-reduce.5.cloned.1.call-start = ((), (), s32[]{:S(2)}) async-start(), calls=%async_computation.8 | async-start | bytes 8388608 | tf_op jit(solution)/shard_map/psum | solution.py:48
  16.6 152.9 %reduce-scatter.13.cloned.1.call-start = ((), (), s32[]{:S(2)}) async-start(), calls=%async_computation.12 | async-start | bytes 2228224 | tf_op jit(solution)/shard_map/reduce_scatter | solution.py:61
  95.1 158.0 %all-reduce.7.cloned.1.call-start = ((), (), s32[]{:S(2)}) async-start(), calls=%async_computation.9 | async-start | bytes 2097152 | tf_op jit(solution)/shard_map/psum | solution.py:57
  191.3 139.9 %reduce-scatter.15.cloned.1.call-start = ((), (), s32[]{:S(2)}) async-start(), calls=%async_computation.13 | async-start | bytes 2228224 | tf_op jit(solution)/shard_map/reduce_scatter | solution.py:61
  257.5 159.0 %all-reduce.9.cloned.1.call-start = ((), (), s32[]{:S(2)}) async-start(), calls=%async_computation.10 | async-start | bytes 2097152 | tf_op jit(solution)/shard_map/psum | solution.py:57
  332.3 84.1 %copy-start = (bf16[4,256,512]{2,1,0:T(8,128)(2,1)S(1)}, bf16[4,256,512]{2,1,0:T(8,128)(2,1)}, u32[]{:S(2)}) copy-start(bf16[4,256,512]{2,1,0:T(8,128)(2,1)} %param.10) | copy-start | bytes 3145732
  354.7 142.3 %reduce-scatter.17.cloned.1.call-start = ((), (), s32[]{:S(2)}) async-start(), calls=%async_computation.14 | async-start | bytes 2228224 | tf_op jit(solution)/shard_map/reduce_scatter | solution.py:61
  423.1 160.3 %all-reduce.11.cloned.1.call-start = ((), (), s32[]{:S(2)}) async-start(), calls=%async_computation.11 | async-start | bytes 2097152 | tf_op jit(solution)/shard_map/psum | solution.py:57
  521.7 140.0 %reduce-scatter.19.cloned.1.call-start = ((), (), s32[]{:S(2)}) async-start(), calls=%async_computation.15 | async-start | bytes 2228224
  585.9 1.9 copy-start.4
  585.9 2.4 copy-start.1
  585.9 2.6 copy-start.2
  585.9 2.8 copy-start.3
Sparse Core Ops, SparseCore 0:
  16.7 74.4 all-reduce.4
  95.2 74.2 reduce-scatter.12
  191.5 61.5 all-reduce.6
  257.6 73.6 reduce-scatter.14
  354.8 61.5 all-reduce.8
  423.2 73.7 reduce-scatter.16
  521.8 61.5 all-reduce.10
  588.0 73.6 reduce-scatter.18
